TPU v7x, 32 devices: a whole 2x2x4 slice. The times are simulated.
32 devices in a mesh: samp: 8 (over z, core), chan: 4 (over y, x).
Axes of the slice: x: 2, y: 2, z: 4, core: 2. Of those that a mesh axis runs over, the one named last changes fastest.
Arguments:
- out_cot: bfloat16 [8, 256, 4096], P('samp', 'chan'), may hold values from -6 to 6
- mix_weight: bfloat16 [256, 256], replicated, may hold values from -0.375 to 0.375
- corr_kernels: float32 [2, 12, 256, 64], P(None, None, 'chan'), may hold values from -0.75 to 0.75
- momentum: int32 [8], P('samp'), may hold values from 0 to 11
- spin_up: int32 [8, 4096], P('samp', 'chan'), may hold values 0 or 1
- layer_input: bfloat16 [8, 256, 4096], P('samp', None, 'chan'), may hold values from -6 to 6
- pre_one: bfloat16 [8, 256, 4096], P('samp', None, 'chan'), may hold values from -6 to 6
- pre_two: bfloat16 [8, 256, 4096], P('samp', None, 'chan'), may hold values from -6 to 6
- conv_weight: bfloat16 [3, 9, 256, 256], replicated, may hold values from -0.125 to 0.125
- dilation: int32 [3, 256], replicated, may hold values from 1 to 4, as said below
Outputs:
- input_grad: bfloat16 [8, 256, 4096], P('samp', None, 'chan')
- weight_grad: float32 [3, 9, 256, 256], P(None, None, 'chan')
Inputs may be any that keep to these rules, and one draw needn't show every extreme that they name: Some channel of every convolution has dilation 4.
All inputs are finite; a program needn't handle non-finite values. No bound on the sum of `spin_up` on one device may be relied on, other than what follows from the above.
Results may differ from a plain program's by a relative error of at most 0.02.
Values may be sent and summed in bfloat16 or wider, within the bound.
A program may use at most 64 MiB of HBM per device.

v0:
```python
import math
import jax
import jax.numpy as jnp
from jax import lax
from jax.sharding import PartitionSpec as P

SIDE = 64
LAYERS = 3
MAXDIL = 4


def with_halo(shard, sides, width):
    for axis, dim in sides:
        size, length = (lax.axis_size(axis), shard.shape[dim])
        up = [(i, (i + 1) % size) for i in range(size)]
        down = [(j, i) for i, j in up]
        last = lax.slice_in_dim(shard, length - width, length, axis=dim)
        leading = lax.slice_in_dim(shard, 0, width, axis=dim)
        before = lax.ppermute(last, axis, up)
        after = lax.ppermute(leading, axis, down)
        shard = jnp.concatenate([before, shard, after], axis=dim)
    return shard


def column_shift(values, step_size, lattice_side, column):
    if step_size == 0:
        return values
    inside = (column - step_size >= 0) & (column - step_size < lattice_side)
    wrapped = step_size - lattice_side if step_size > 0 else step_size + lattice_side
    return jnp.where(inside, jnp.roll(values, step_size, axis=2), jnp.roll(values, wrapped, axis=2))


def on_device(
    out_cot,
    mix_weight,
    corr_kernels,
    momentum,
    spin_up,
    layer_input,
    pre_one,
    pre_two,
    conv_weight,
    dilation,
):
    highest = lax.Precision.HIGHEST
    sample_count = out_cot.shape[0]
    chan_block = out_cot.shape[1]
    site_count = out_cot.shape[2]
    sectors = corr_kernels.shape[1]
    lattice_side = corr_kernels.shape[3]
    slab_cells = layer_input.shape[2]
    own_start = lax.axis_index("chan") * chan_block
    own_rows = lax.dynamic_slice_in_dim(mix_weight, own_start, chan_block, 0)
    input_cot = lax.psum_scatter(
        jnp.einsum("oc,son->csn", own_rows, out_cot, preferred_element_type=jnp.float32),
        "chan",
        scatter_dimension=0,
        tiled=True,
    )
    onehot = (momentum[:, None] == jnp.arange(sectors, dtype=jnp.int32)[None, :]).astype(
        jnp.float32
    )
    picked = jnp.einsum("sk,akci->acsi", onehot, corr_kernels, precision=highest)
    positions = jnp.arange(lattice_side, dtype=jnp.int32)
    circ_table = (
        (positions[None, None, :] - positions[None, :, None]) % lattice_side
        == positions[:, None, None]
    ).astype(jnp.float32)
    circulant = jnp.einsum("acsi,ixy->acsxy", picked, circ_table, precision=highest)
    grid_values = input_cot.reshape(chan_block, sample_count, lattice_side, lattice_side)
    halfway = jnp.einsum("csxX,csxy->csXy", circulant[0], grid_values, precision=highest)
    corr_grad = jnp.einsum("csXy,csyY->scXY", halfway, circulant[1], precision=highest)
    corr_grad = corr_grad.reshape(sample_count, chan_block, site_count).astype(jnp.bfloat16)
    regrouped = lax.all_to_all(corr_grad, "chan", split_axis=2, concat_axis=1, tiled=True)
    spin_gate = jnp.where(spin_up == 1, 1.5, 0.5).astype(jnp.float32)[:, None, :]
    grad_now = (regrouped.astype(jnp.float32) * spin_gate).astype(jnp.bfloat16)
    halo_cells = MAXDIL * SIDE
    column = jnp.arange(slab_cells, dtype=jnp.int32) % lattice_side
    norm_factor = 1.0 / math.sqrt(sample_count * lax.axis_size("samp") * site_count)
    layer_grads = [None] * LAYERS
    input_grad = None
    for conv_level in range(LAYERS - 1, -1, -1):
        slope_base = None
        if conv_level == 0:
            layer_values = layer_input
        else:
            saved_pre = pre_one if conv_level == 1 else pre_two
            slope_base = jnp.tanh(saved_pre.astype(jnp.float32))
            layer_values = slope_base.astype(jnp.bfloat16)
        padded = with_halo(grad_now, (("chan", 2),), halo_cells)
        back_sum = jnp.zeros(grad_now.shape, jnp.float32)
        tap_grads = []
        for row_step in (-1, 0, 1):
            for col_step in (-1, 0, 1):
                tap_index = (row_step + 1) * 3 + col_step + 1
                if row_step == 0 and col_step == 0:
                    combined = grad_now
                else:
                    combined = None
                    for dilate in range(1, MAXDIL + 1):
                        slice_begin = halo_cells - row_step * dilate * lattice_side
                        shifted = column_shift(
                            padded[:, :, slice_begin : slice_begin + slab_cells],
                            col_step * dilate,
                            lattice_side,
                            column,
                        )
                        if combined is None:
                            combined = shifted
                        else:
                            chosen_mask = (dilation[conv_level] == dilate)[None, :, None]
                            combined = jnp.where(chosen_mask, shifted, combined)
                back_sum = back_sum + jnp.einsum(
                    "oc,son->scn",
                    conv_weight[conv_level, tap_index],
                    combined,
                    preferred_element_type=jnp.float32,
                )
                tap_grads.append(
                    jnp.einsum(
                        "son,scn->oc", combined, layer_values, preferred_element_type=jnp.float32
                    )
                    * norm_factor
                )
        local_grad = jnp.stack(tap_grads)
        reduced = lax.psum_scatter(
            local_grad.astype(jnp.bfloat16), "chan", scatter_dimension=1, tiled=True
        )
        layer_grads[conv_level] = lax.psum(reduced, "samp").astype(jnp.float32)
        if conv_level > 0:
            grad_now = (back_sum * (1.0 - slope_base * slope_base)).astype(jnp.bfloat16)
        else:
            input_grad = back_sum.astype(jnp.bfloat16)
    weight_grad = jnp.stack(layer_grads)
    return (input_grad, weight_grad)


def solution(mesh):
    in_specs = (
        P("samp", "chan", None),
        P(),
        P(None, None, "chan", None),
        P("samp"),
        P("samp", "chan"),
        P("samp", None, "chan"),
        P("samp", None, "chan"),
        P("samp", None, "chan"),
        P(),
        P(),
    )
    out_specs = (P("samp", None, "chan"), P(None, None, "chan", None))
    return jax.shard_map(
        on_device, mesh=mesh, in_specs=in_specs, out_specs=out_specs, check_vma=False
    )
```

profile of v0, /device:TPU:0, one launch (start us, length us, event | category | flops | bytes accessed | tf_op | source)
XLA Modules:
  0.0 344.3 jit_solution(6769106226334867354)
XLA Ops:
  7.2 3.8 %convolution_bitcast_fusion = f32[256,1,4096]{2,0,1:T(8,128)} fusion(bf16[1,64,4096]{2,1,0:T(8,128)(2,1)} %param.10, bf16[256,256]{1,0:T(8,128)(2,1)} %param.11, s32[]{:T(128)S(6)} %select_n.3285), kind=kOutput, calls=%fused_computation | convolution fusion | flops 134217728 | bytes 4751364 | tf_op jit(solution)/shard_map/oc,son->csn/dot_general | solution.py:55
  16.8 49.8 %reduce-scatter.5.cloned.1.call-done = f32[64,1,4096]{2,0,1:T(8,128)} async-done(((f32[256,1,4096]{2,0,1:T(8,128)}), f32[64,1,4096]{2,0,1:T(8,128)}) %reduce-scatter.5.cloned.1.call-update) | async-done | bytes 1048592 | tf_op jit(solution)/shard_map/reduce_scatter | solution.py:54
  68.8 6.2 %fusion.2 = f32[64,64,64]{2,1,0:T(8,128)S(1)} fusion(f32[64,64,64]{2,1,0:T(8,128)S(1)} %reshape.16731, f32[64,64,64]{2,0,1:T(8,128)} %get-tuple-element.25), kind=kOutput, calls=%fused_computation.119 | convolution fusion | flops 201326592 | bytes 3145728 | tf_op jit(solution)/shard_map/csxX,csxy->csXy/dot_general | solution.py:71
  75.0 3.3 fusion.7
  82.5 23.6 %reduce.18 = bf16[4096,64]{1,0:T(8,128)(2,1)} reduce(bf16[4096,1,64]{2,1,0:T(2,128)(2,1)S(1)} %bitcast.976, bf16[]{:T(256)} %broadcast.4323), dimensions={1}, to_apply=%bitcast.918.reduce_sub_computation | reduce | bytes 1048578
  108.7 3.5 %all-to-all-start = ((bf16[4,2,32768]{2,1,0:T(2,128)(2,1)}), bf16[4,2,32768]{2,1,0:T(2,128)(2,1)S(1)}, u32[]{:S(2)}, u32[]{:S(2)}) async-start(bf16[4,2,32768]{2,1,0:T(2,128)(2,1)} %reshape.16776), calls=%async_computation.1 | async-start | bytes 1048576 | tf_op jit(solution)/shard_map/all_to_all | solution.py:74
  114.4 6.1 %all-to-all-done = bf16[4,2,32768]{2,1,0:T(2,128)(2,1)S(1)} async-done(((bf16[4,2,32768]{2,1,0:T(2,128)(2,1)}), bf16[4,2,32768]{2,1,0:T(2,128)(2,1)S(1)}, u32[]{:S(2)}, u32[]{:S(2)}) %all-to-all-start) | async-done | bytes 524320 | tf_op jit(solution)/shard_map/all_to_all | solution.py:74
  129.6 4.8 %collective-permute-done = bf16[1,256,256]{1,2,0:T(8,128)(2,1)S(1)} collective-permute-done((bf16[1,256,256]{1,2,0:T(8,128)(2,1)S(1)}, bf16[1,256,256]{1,2,0:T(8,128)(2,1)S(1)}, u32[]{:S(2)}, u32[]{:S(2)}) %collective-permute-start) | collective-permute-done | bytes 131104 | tf_op jit(solution)/shard_map/ppermute | solution.py:20
  137.4 3.0 fusion.252
  143.4 3.0 fusion.256
  147.6 3.0 fusion.260
  153.1 3.0 fusion.264
  157.4 3.0 fusion.268
  162.9 3.0 fusion.272
  177.7 3.0 fusion.276
  183.7 3.0 fusion.280
  187.9 3.0 fusion.284
  193.4 3.0 fusion.288
  197.6 3.0 fusion.292
  203.1 3.0 fusion.296
  218.1 3.0 fusion.300
  223.8 3.0 fusion.304
  254.7 20.1 %reduce-scatter.7.cloned.1.call-done = bf16[9,64,256]{2,1,0:T(8,128)(2,1)} async-done(((bf16[9,256,256]{2,1,0:T(8,128)(2,1)}), bf16[9,64,256]{2,1,0:T(8,128)(2,1)}) %reduce-scatter.7.cloned.1.call-update) | async-done | bytes 294928 | tf_op jit(solution)/shard_map/reduce_scatter | solution.py:126
  278.4 56.7 %all-reduce.3.cloned.1.call-done = (bf16[1,9,64,256]{3,2,1,0:T(8,128)(2,1)}, bf16[1,9,64,256]{3,2,1,0:T(8,128)(2,1)}, bf16[1,9,64,256]{3,2,1,0:T(8,128)(2,1)}) async-done(((bf16[1,9,64,256]{3,2,1,0:T(8,128)(2,1)}, bf16[1,9,64,256]{3,2,1,0:T(8,128)(2,1)}, bf16[1,9,64,256]{3,2,1,0:T(8,128)(2,1)}), (bf16[1,9,64,256]{3,2,1,0:T(8,128)(2,1)}, bf16[1,9,64,256]{3,2,1,0:T(8,128)(2,1)}, ...) | async-done | bytes 884752 | tf_op jit(solution)/shard_map/psum | solution.py:129
  (250 shorter events, 108.0 us)
Async XLA Ops:
  7.2 4.7 %copy-start = (f32[2,12,64,64]{3,2,1,0:T(8,128)S(1)}, f32[2,12,64,64]{3,2,1,0:T(8,128)}, u32[]{:S(2)}) copy-start(f32[2,12,64,64]{3,2,1,0:T(8,128)} %param.12) | copy-start | bytes 1179652
  7.2 59.5 %reduce-scatter.5.cloned.1.call-start = ((), (), s32[]{:S(2)}) async-start(), calls=%async_computation.5 | async-start | bytes 5242880 | tf_op jit(solution)/shard_map/reduce_scatter | solution.py:54
  68.8 6.2 %copy-start.2 = (f32[64,64,64]{2,0,1:T(8,128)S(1)}, f32[64,64,64]{2,0,1:T(8,128)}, u32[]{:S(2)}) copy-start(f32[64,64,64]{2,0,1:T(8,128)} %get-tuple-element.24) | copy-start | bytes 3145732
  106.1 6.2 %copy-start.15 = (bf16[1,256,1024]{2,1,0:T(8,128)(2,1)S(1)}, bf16[1,256,1024]{2,1,0:T(8,128)(2,1)}, u32[]{:S(2)}) copy-start(bf16[1,256,1024]{2,1,0:T(8,128)(2,1)} %param.16) | copy-start | bytes 1572868
  106.1 7.2 %copy-start.16 = (bf16[1,256,1024]{2,1,0:T(8,128)(2,1)S(1)}, bf16[1,256,1024]{2,1,0:T(8,128)(2,1)}, u32[]{:S(2)}) copy-start(bf16[1,256,1024]{2,1,0:T(8,128)(2,1)} %param.17) | copy-start | bytes 1572868
  106.1 8.2 %copy-start.18 = (s32[3,256]{1,0:T(4,128)S(1)}, s32[3,256]{1,0:T(4,128)}, u32[]{:S(2)}) copy-start(s32[3,256]{1,0:T(4,128)} %param.19) | copy-start | bytes 9220
  106.1 8.3 %copy-start.17 = (s32[1,1024]{1,0:T(1,128)S(1)}, s32[1,1024]{1,0:T(1,128)}, u32[]{:S(2)}) copy-start(s32[1,1024]{1,0:T(1,128)} %param.14) | copy-start | bytes 12292
  108.7 11.7 %all-to-all-start = ((bf16[4,2,32768]{2,1,0:T(2,128)(2,1)}), bf16[4,2,32768]{2,1,0:T(2,128)(2,1)S(1)}, u32[]{:S(2)}, u32[]{:S(2)}) async-start(bf16[4,2,32768]{2,1,0:T(2,128)(2,1)} %reshape.16776), calls=%async_computation.1 | async-start | bytes 1048576 | tf_op jit(solution)/shard_map/all_to_all | solution.py:74
  112.2 142.5 %reduce-scatter.11.cloned.1.call-start = ((), (), s32[]{:S(2)}) async-start(), calls=%async_computation.8 | async-start | bytes 1474560 | tf_op jit(solution)/shard_map/reduce_scatter | solution.py:126
  126.2 8.3 %collective-permute-start.1 = (bf16[1,256,256]{1,2,0:T(8,128)(2,1)S(1)}, bf16[1,256,256]{1,2,0:T(8,128)(2,1)S(1)}, u32[]{:S(2)}, u32[]{:S(2)}) collective-permute-start(bf16[1,256,256]{1,2,0:T(8,128)(2,1)S(1)} %get-tuple-element.324), channel_id=1, source_target_pairs={{0,1},{1,2},{2,3},{3,0},{4,5},{5,6},{6,7},{7,4},{8,9},{9,10},{10,1... | collective-permute-start | bytes 393224 | tf_op jit(solution)/shard_map/ppermute | solution.py:19
  127.7 6.7 %collective-permute-start = (bf16[1,256,256]{1,2,0:T(8,128)(2,1)S(1)}, bf16[1,256,256]{1,2,0:T(8,128)(2,1)S(1)}, u32[]{:S(2)}, u32[]{:S(2)}) collective-permute-start(bf16[1,256,256]{1,2,0:T(8,128)(2,1)S(1)} %get-tuple-element.325), channel_id=1, source_target_pairs={{1,0},{2,1},{3,2},{0,3},{5,4},{6,5},{7,6},{4,7},{9,8},{10,9},{11,1... | collective-permute-start | bytes 393224 | tf_op jit(solution)/shard_map/ppermute | solution.py:20
  167.7 7.3 %collective-permute-start.3 = (bf16[1,256,256]{1,2,0:T(8,128)(2,1)S(1)}, bf16[1,256,256]{1,2,0:T(8,128)(2,1)S(1)}, u32[]{:S(2)}, u32[]{:S(2)}) collective-permute-start(bf16[1,256,256]{1,2,0:T(8,128)(2,1)S(1)} %get-tuple-element.258), channel_id=1, source_target_pairs={{0,1},{1,2},{2,3},{3,0},{4,5},{5,6},{6,7},{7,4},{8,9},{9,10},{10,1... | collective-permute-start | bytes 393224 | tf_op jit(solution)/shard_map/ppermute | solution.py:19
  168.8 6.1 %collective-permute-start.2 = (bf16[1,256,256]{1,2,0:T(8,128)(2,1)S(1)}, bf16[1,256,256]{1,2,0:T(8,128)(2,1)S(1)}, u32[]{:S(2)}, u32[]{:S(2)}) collective-permute-start(bf16[1,256,256]{1,2,0:T(8,128)(2,1)S(1)} %get-tuple-element.259), channel_id=1, source_target_pairs={{1,0},{2,1},{3,2},{0,3},{5,4},{6,5},{7,6},{4,7},{9,8},{10,9},{11,1... | collective-permute-start | bytes 393224 | tf_op jit(solution)/shard_map/ppermute | solution.py:20
  174.8 79.9 %reduce-scatter.9.cloned.1.call-start = ((), (), s32[]{:S(2)}) async-start(), calls=%async_computation.7 | async-start | bytes 1474560 | tf_op jit(solution)/shard_map/reduce_scatter | solution.py:126
  207.6 7.8 %collective-permute-start.5 = (bf16[1,256,256]{1,2,0:T(8,128)(2,1)S(1)}, bf16[1,256,256]{1,2,0:T(8,128)(2,1)S(1)}, u32[]{:S(2)}, u32[]{:S(2)}) collective-permute-start(bf16[1,256,256]{1,2,0:T(8,128)(2,1)S(1)} %get-tuple-element.192), channel_id=1, source_target_pairs={{0,1},{1,2},{2,3},{3,0},{4,5},{5,6},{6,7},{7,4},{8,9},{9,10},{10,1... | collective-permute-start | bytes 393224 | tf_op jit(solution)/shard_map/ppermute | solution.py:19
  208.5 6.8 %collective-permute-start.4 = (bf16[1,256,256]{1,2,0:T(8,128)(2,1)S(1)}, bf16[1,256,256]{1,2,0:T(8,128)(2,1)S(1)}, u32[]{:S(2)}, u32[]{:S(2)}) collective-permute-start(bf16[1,256,256]{1,2,0:T(8,128)(2,1)S(1)} %get-tuple-element.193), channel_id=1, source_target_pairs={{1,0},{2,1},{3,2},{0,3},{5,4},{6,5},{7,6},{4,7},{9,8},{10,9},{11,1... | collective-permute-start | bytes 393224 | tf_op jit(solution)/shard_map/ppermute | solution.py:20
  215.0 59.8 %reduce-scatter.7.cloned.1.call-start = ((), (), s32[]{:S(2)}) async-start(), calls=%async_computation.6 | async-start | bytes 1474560 | tf_op jit(solution)/shard_map/reduce_scatter | solution.py:126
  218.1 3.0 copy-start.19
  222.7 4.1 %copy-start.11 = (bf16[256,1024]{0,1:T(8,128)(2,1)}, bf16[256,1024]{0,1:T(8,128)(2,1)S(1)}, u32[]{:S(2)}) copy-start(bf16[256,1024]{0,1:T(8,128)(2,1)S(1)} %get-tuple-element.123) | copy-start | bytes 1572868
  222.7 18.2 %copy-start.9 = (bf16[256,1024]{0,1:T(8,128)(2,1)}, bf16[256,1024]{0,1:T(8,128)(2,1)S(1)}, u32[]{:S(2)}) copy-start(bf16[256,1024]{0,1:T(8,128)(2,1)S(1)} %get-tuple-element.122) | copy-start | bytes 1572868
  235.8 4.0 %copy-start.3 = (bf16[256,1024]{0,1:T(8,128)(2,1)}, bf16[256,1024]{0,1:T(8,128)(2,1)S(1)}, u32[]{:S(2)}) copy-start(bf16[256,1024]{0,1:T(8,128)(2,1)S(1)} %fusion.312) | copy-start | bytes 1572868
  245.9 89.1 %all-reduce.3.cloned.1.call-start = ((), (), s32[]{:S(2)}) async-start(), calls=%async_computation.9 | async-start | bytes 1769472 | tf_op jit(solution)/shard_map/psum | solution.py:129
  253.4 21.5 %copy-start.10 = (bf16[256,1024]{0,1:T(8,128)(2,1)S(1)}, bf16[256,1024]{0,1:T(8,128)(2,1)}, u32[]{:S(2)}) copy-start(bf16[256,1024]{0,1:T(8,128)(2,1)} %copy-done.9) | copy-start | bytes 1572868
  276.1 61.5 %copy-start.1 = (f32[2,12,64,64]{3,2,1,0:T(8,128)S(1)}, f32[2,12,64,64]{3,2,1,0:T(8,128)}, u32[]{:S(2)}) copy-start(f32[2,12,64,64]{3,2,1,0:T(8,128)} %param.12) | copy-start | bytes 1179652
  (8 other events, 17.5 us)
Sparse Core Ops, SparseCore 0:
  11.2 55.3 reduce-scatter.4
  174.9 27.8 reduce-scatter.10
  215.1 28.0 reduce-scatter.8
  246.3 28.5 reduce-scatter.6
  277.4 57.5 all-reduce.2
where the time goes:
time: 348 us; the launch traced here: 344 us
  waiting for transfers between devices  138 us (40%)
  other arithmetic  90.3 us (26%)
  matrix products  64.6 us (19%)
  local copies, waits for them, and re-layouts  22.2 us (6%)
  between operations  16.2 us (5%)
  starting transfers between devices  13.4 us (4%)
    psum x1, waiting for transfers between devices, on_device(): layer_grads[conv_level] = lax.psum(reduced, 'samp').astype(jnp.float32)  56.7 us
    select_n x18, other arithmetic, on_device(): combined = jnp.where(chosen_mask, shifted, combined)  54 us
    reduce_scatter x1, waiting for transfers between devices, on_device(): lax.psum_scatter(jnp.einsum('oc,son->csn', own_rows, out_cot, preferred_e...  49.8 us
    dot_general x27, matrix products, on_device(): jnp.einsum('oc,son->scn', conv_weight[conv_level, tap_index], combined, p...  32.9 us
    unnamed x1, other arithmetic  23.6 us
    reduce_scatter x3, waiting for transfers between devices, on_device(): lax.psum_scatter(local_grad.astype(jnp.bfloat16), 'chan', scatter_dimensi...  20.1 us
    dot_general x27, matrix products, on_device(): jnp.einsum('son,scn->oc', combined, layer_values, preferred_element_type=...  15.7 us
    unnamed x46, local copies, waits for them, and re-layouts  9.22 us
  transfers between devices with their start and end apart: 12, of which 5 were waited for; matrix products, arithmetic and copies ran while one was open for 26% of the time, Pallas kernels for 0%

commit v1 on v0

--- a/solution.py
+++ b/solution.py
@@ -3,6 +3,7 @@
 import jax.numpy as jnp
 from jax import lax
 from jax.sharding import PartitionSpec as P
+from jax.lax import all_to_all, axis_size
 
 SIDE = 64
 LAYERS = 3
@@ -71,7 +72,13 @@
     halfway = jnp.einsum("csxX,csxy->csXy", circulant[0], grid_values, precision=highest)
     corr_grad = jnp.einsum("csXy,csyY->scXY", halfway, circulant[1], precision=highest)
     corr_grad = corr_grad.reshape(sample_count, chan_block, site_count).astype(jnp.bfloat16)
-    regrouped = lax.all_to_all(corr_grad, "chan", split_axis=2, concat_axis=1, tiled=True)
+    low = all_to_all(
+        jnp.stack(jnp.split(corr_grad, axis_size("chan"), axis=2), axis=0),
+        split_axis=0,
+        axis_name="chan",
+        concat_axis=0,
+    )
+    regrouped = jnp.concatenate(low, axis=1)
     spin_gate = jnp.where(spin_up == 1, 1.5, 0.5).astype(jnp.float32)[:, None, :]
     grad_now = (regrouped.astype(jnp.float32) * spin_gate).astype(jnp.bfloat16)
     halo_cells = MAXDIL * SIDE

time: 348 us -> 328 us (0.943)
  other arithmetic: 90.3 us -> 67.9 us
  matrix products: 64.6 us -> 76.5 us
  local copies, waits for them, and re-layouts: 22.2 us -> 13.4 us
    unnamed x1 -> x0, other arithmetic: 23.6 us -> none
    dot_general x27, matrix products: 15.7 us -> 27.6 us  [on_device(): jnp.einsum('son,scn->oc', combined, layer_values, preferred_element_type=...]
    unnamed x46 -> x91, local copies, waits for them, and re-layouts: 9.22 us -> 2.81 us
  transfers between devices with their start and end apart: 12 -> 12, of which waited for: 5 -> 5; matrix products, arithmetic and copies ran while one was open for 26% -> 32% of each run, Pallas kernels for 0% -> 0%
where the time goes in v1:
time: 328 us; the launch traced here: 324 us
  waiting for transfers between devices  137 us (42%)
  matrix products  76.5 us (23%)
  other arithmetic  67.9 us (21%)
  between operations  16.4 us (5%)
  local copies, waits for them, and re-layouts  13.4 us (4%)
  starting transfers between devices  13.2 us (4%)
    psum x1, waiting for transfers between devices, on_device(): layer_grads[conv_level] = lax.psum(reduced, 'samp').astype(jnp.float32)  56.6 us
    select_n x18, other arithmetic, on_device(): combined = jnp.where(chosen_mask, shifted, combined)  54 us
    reduce_scatter x1, waiting for transfers between devices, on_device(): lax.psum_scatter(jnp.einsum('oc,son->csn', own_rows, out_cot, preferred_e...  49.8 us
    dot_general x27, matrix products, on_device(): jnp.einsum('oc,son->scn', conv_weight[conv_level, tap_index], combined, p...  32.8 us
    dot_general x27, matrix products, on_device(): jnp.einsum('son,scn->oc', combined, layer_values, preferred_element_type=...  27.6 us
    reduce_scatter x3, waiting for transfers between devices, on_device(): lax.psum_scatter(local_grad.astype(jnp.bfloat16), 'chan', scatter_dimensi...  19.2 us
    ppermute x3, starting transfers between devices, with_halo(): after = lax.ppermute(leading, axis, down)  6.68 us
  transfers between devices with their start and end apart: 12, of which 5 were waited for; matrix products, arithmetic and copies ran while one was open for 32% of the time, Pallas kernels for 0%

profile of v1, /device:TPU:0, one launch (start us, length us, event | category | flops | bytes accessed | tf_op | source)
XLA Modules:
  0.0 324.1 jit_solution(8321915427252353210)
XLA Ops:
  7.2 3.9 %convolution_bitcast_fusion = f32[256,1,4096]{2,0,1:T(8,128)} fusion(bf16[1,64,4096]{2,1,0:T(8,128)(2,1)} %param.10, bf16[256,256]{1,0:T(8,128)(2,1)} %param.11, s32[]{:T(128)S(6)} %select_n.3285), kind=kOutput, calls=%fused_computation | convolution fusion | flops 134217728 | bytes 4751364 | tf_op jit(solution)/shard_map/oc,son->csn/dot_general | solution.py:56
  16.9 49.8 %reduce-scatter.5.cloned.1.call-done = f32[64,1,4096]{2,0,1:T(8,128)} async-done(((f32[256,1,4096]{2,0,1:T(8,128)}), f32[64,1,4096]{2,0,1:T(8,128)}) %reduce-scatter.5.cloned.1.call-update) | async-done | bytes 1048592 | tf_op jit(solution)/shard_map/reduce_scatter | solution.py:55
  68.9 6.2 %fusion.2 = f32[64,64,64]{2,1,0:T(8,128)S(1)} fusion(f32[64,64,64]{2,1,0:T(8,128)S(1)} %reshape.16728, f32[64,64,64]{2,0,1:T(8,128)} %get-tuple-element.21), kind=kOutput, calls=%fused_computation.119 | convolution fusion | flops 201326592 | bytes 3145728 | tf_op jit(solution)/shard_map/csxX,csxy->csXy/dot_general | solution.py:72
  75.0 3.3 %fusion.7 = bf16[64,64,64]{2,1,0:T(8,128)(2,1)S(1)} fusion(f32[64,64,64]{2,1,0:T(8,128)S(1)} %fusion.2, f32[64,64,64]{2,0,1:T(8,128)S(1)} %copy-done.2), kind=kOutput, calls=%fused_computation.124 | convolution fusion | flops 201588736 | bytes 2621440 | tf_op jit(solution)/shard_map/csXy,csyY->scXY/dot_general | solution.py:73
  80.2 3.5 %all-to-all-start = ((bf16[4,1,64,1024]{3,2,1,0:T(8,128)(2,1)}), bf16[4,1,64,1024]{3,2,1,0:T(8,128)(2,1)S(1)}, u32[]{:S(2)}, u32[]{:S(2)}) async-start(bf16[4,1,64,1024]{3,2,1,0:T(8,128)(2,1)} %pad_maximum_fusion), calls=%async_computation.1 | async-start | bytes 1048576 | tf_op jit(solution)/shard_map/all_to_all | solution.py:75
  85.5 6.4 %all-to-all-done = bf16[4,1,64,1024]{3,2,1,0:T(8,128)(2,1)S(1)} async-done(((bf16[4,1,64,1024]{3,2,1,0:T(8,128)(2,1)}), bf16[4,1,64,1024]{3,2,1,0:T(8,128)(2,1)S(1)}, u32[]{:S(2)}, u32[]{:S(2)}) %all-to-all-start) | async-done | bytes 524320 | tf_op jit(solution)/shard_map/all_to_all | solution.py:75
  96.2 4.7 %collective-permute-done = bf16[1,256,256]{1,2,0:T(8,128)(2,1)S(1)} collective-permute-done((bf16[1,256,256]{1,2,0:T(8,128)(2,1)S(1)}, bf16[1,256,256]{1,2,0:T(8,128)(2,1)S(1)}, u32[]{:S(2)}, u32[]{:S(2)}) %collective-permute-start) | collective-permute-done | bytes 131104 | tf_op jit(solution)/shard_map/ppermute | solution.py:21
  103.8 3.0 fusion.251
  109.7 3.0 fusion.255
  113.9 3.0 fusion.259
  119.4 3.0 fusion.263
  123.7 3.0 fusion.267
  129.2 3.0 fusion.271
  148.9 3.0 fusion.275
  154.9 3.0 fusion.279
  159.1 3.0 fusion.283
  164.5 3.0 fusion.287
  168.8 3.0 fusion.291
  174.3 3.0 fusion.295
  198.7 3.0 fusion.299
  204.4 3.0 fusion.303
  208.5 3.0 fusion.307
  235.5 19.1 %reduce-scatter.7.cloned.1.call-done = bf16[9,64,256]{2,1,0:T(8,128)(2,1)} async-done(((bf16[9,256,256]{2,1,0:T(8,128)(2,1)}), bf16[9,64,256]{2,1,0:T(8,128)(2,1)}) %reduce-scatter.7.cloned.1.call-update) | async-done | bytes 294928 | tf_op jit(solution)/shard_map/reduce_scatter | solution.py:133
  258.2 56.6 %all-reduce.3.cloned.1.call-done = (bf16[1,9,64,256]{3,2,1,0:T(8,128)(2,1)}, bf16[1,9,64,256]{3,2,1,0:T(8,128)(2,1)}, bf16[1,9,64,256]{3,2,1,0:T(8,128)(2,1)}) async-done(((bf16[1,9,64,256]{3,2,1,0:T(8,128)(2,1)}, bf16[1,9,64,256]{3,2,1,0:T(8,128)(2,1)}, bf16[1,9,64,256]{3,2,1,0:T(8,128)(2,1)}), (bf16[1,9,64,256]{3,2,1,0:T(8,128)(2,1)}, bf16[1,9,64,256]{3,2,1,0:T(8,128)(2,1)}, ...) | async-done | bytes 884752 | tf_op jit(solution)/shard_map/psum | solution.py:136
  (292 shorter events, 109.2 us)
Async XLA Ops:
  7.2 4.7 %copy-start = (f32[2,12,64,64]{3,2,1,0:T(8,128)S(1)}, f32[2,12,64,64]{3,2,1,0:T(8,128)}, u32[]{:S(2)}) copy-start(f32[2,12,64,64]{3,2,1,0:T(8,128)} %param.12) | copy-start | bytes 1179652
  7.2 59.5 %reduce-scatter.5.cloned.1.call-start = ((), (), s32[]{:S(2)}) async-start(), calls=%async_computation.5 | async-start | bytes 5242880 | tf_op jit(solution)/shard_map/reduce_scatter | solution.py:55
  11.8 157.0 %copy-start.18 = (pred[1024]{0:T(1024)(128)(4,1)}, pred[1024]{0:T(1024)(128)(4,1)S(1)}, u32[]{:S(2)}) copy-start(pred[1024]{0:T(1024)(128)(4,1)S(1)} %get-tuple-element.326) | copy-start | bytes 3076
  11.8 157.0 %copy-start.20 = (pred[1024]{0:T(1024)(128)(4,1)}, pred[1024]{0:T(1024)(128)(4,1)S(1)}, u32[]{:S(2)}) copy-start(pred[1024]{0:T(1024)(128)(4,1)S(1)} %get-tuple-element.327) | copy-start | bytes 3076
  68.9 6.2 %copy-start.2 = (f32[64,64,64]{2,0,1:T(8,128)S(1)}, f32[64,64,64]{2,0,1:T(8,128)}, u32[]{:S(2)}) copy-start(f32[64,64,64]{2,0,1:T(8,128)} %get-tuple-element.20) | copy-start | bytes 3145732
  78.4 5.3 %copy-start.12 = (bf16[1,256,1024]{2,1,0:T(8,128)(2,1)S(1)}, bf16[1,256,1024]{2,1,0:T(8,128)(2,1)}, u32[]{:S(2)}) copy-start(bf16[1,256,1024]{2,1,0:T(8,128)(2,1)} %param.16) | copy-start | bytes 1572868
  79.3 5.7 %copy-start.42 = (s32[3,256]{1,0:T(4,128)S(1)}, s32[3,256]{1,0:T(4,128)}, u32[]{:S(2)}) copy-start(s32[3,256]{1,0:T(4,128)} %param.19) | copy-start | bytes 9220
  79.3 6.2 %copy-start.41 = (s32[1,1024]{1,0:T(1,128)S(1)}, s32[1,1024]{1,0:T(1,128)}, u32[]{:S(2)}) copy-start(s32[1,1024]{1,0:T(1,128)} %param.14) | copy-start | bytes 12292
  80.2 11.7 %all-to-all-start = ((bf16[4,1,64,1024]{3,2,1,0:T(8,128)(2,1)}), bf16[4,1,64,1024]{3,2,1,0:T(8,128)(2,1)S(1)}, u32[]{:S(2)}, u32[]{:S(2)}) async-start(bf16[4,1,64,1024]{3,2,1,0:T(8,128)(2,1)} %pad_maximum_fusion), calls=%async_computation.1 | async-start | bytes 1048576 | tf_op jit(solution)/shard_map/all_to_all | solution.py:75
  83.6 151.9 %reduce-scatter.11.cloned.1.call-start = ((), (), s32[]{:S(2)}) async-start(), calls=%async_computation.8 | async-start | bytes 1474560 | tf_op jit(solution)/shard_map/reduce_scatter | solution.py:133
  83.7 90.6 %copy-start.22 = (pred[1024]{0:T(1024)(128)(4,1)}, pred[1024]{0:T(1024)(128)(4,1)S(1)}, u32[]{:S(2)}) copy-start(pred[1024]{0:T(1024)(128)(4,1)S(1)} %get-tuple-element.330) | copy-start | bytes 3076
  83.7 90.6 %copy-start.24 = (pred[1024]{0:T(1024)(128)(4,1)}, pred[1024]{0:T(1024)(128)(4,1)S(1)}, u32[]{:S(2)}) copy-start(pred[1024]{0:T(1024)(128)(4,1)S(1)} %get-tuple-element.331) | copy-start | bytes 3076
  92.8 8.3 %collective-permute-start.1 = (bf16[1,256,256]{1,2,0:T(8,128)(2,1)S(1)}, bf16[1,256,256]{1,2,0:T(8,128)(2,1)S(1)}, u32[]{:S(2)}, u32[]{:S(2)}) collective-permute-start(bf16[1,256,256]{1,2,0:T(8,128)(2,1)S(1)} %get-tuple-element.320), channel_id=1, source_target_pairs={{0,1},{1,2},{2,3},{3,0},{4,5},{5,6},{6,7},{7,4},{8,9},{9,10},{10,1... | collective-permute-start | bytes 393224 | tf_op jit(solution)/shard_map/ppermute | solution.py:20
  94.2 6.7 %collective-permute-start = (bf16[1,256,256]{1,2,0:T(8,128)(2,1)S(1)}, bf16[1,256,256]{1,2,0:T(8,128)(2,1)S(1)}, u32[]{:S(2)}, u32[]{:S(2)}) collective-permute-start(bf16[1,256,256]{1,2,0:T(8,128)(2,1)S(1)} %get-tuple-element.321), channel_id=1, source_target_pairs={{1,0},{2,1},{3,2},{0,3},{5,4},{6,5},{7,6},{4,7},{9,8},{10,9},{11,1... | collective-permute-start | bytes 393224 | tf_op jit(solution)/shard_map/ppermute | solution.py:21
  134.7 11.5 %collective-permute-start.3 = (bf16[1,256,256]{1,2,0:T(8,128)(2,1)S(1)}, bf16[1,256,256]{1,2,0:T(8,128)(2,1)S(1)}, u32[]{:S(2)}, u32[]{:S(2)}) collective-permute-start(bf16[1,256,256]{1,2,0:T(8,128)(2,1)S(1)} %get-tuple-element.254), channel_id=1, source_target_pairs={{0,1},{1,2},{2,3},{3,0},{4,5},{5,6},{6,7},{7,4},{8,9},{9,10},{10,1... | collective-permute-start | bytes 393224 | tf_op jit(solution)/shard_map/ppermute | solution.py:20
  135.7 10.3 %collective-permute-start.2 = (bf16[1,256,256]{1,2,0:T(8,128)(2,1)S(1)}, bf16[1,256,256]{1,2,0:T(8,128)(2,1)S(1)}, u32[]{:S(2)}, u32[]{:S(2)}) collective-permute-start(bf16[1,256,256]{1,2,0:T(8,128)(2,1)S(1)} %get-tuple-element.255), channel_id=1, source_target_pairs={{1,0},{2,1},{3,2},{0,3},{5,4},{6,5},{7,6},{4,7},{9,8},{10,9},{11,1... | collective-permute-start | bytes 393224 | tf_op jit(solution)/shard_map/ppermute | solution.py:21
  146.0 89.5 %reduce-scatter.9.cloned.1.call-start = ((), (), s32[]{:S(2)}) async-start(), calls=%async_computation.7 | async-start | bytes 1474560 | tf_op jit(solution)/shard_map/reduce_scatter | solution.py:133
  182.9 12.6 %collective-permute-start.5 = (bf16[1,256,256]{1,2,0:T(8,128)(2,1)S(1)}, bf16[1,256,256]{1,2,0:T(8,128)(2,1)S(1)}, u32[]{:S(2)}, u32[]{:S(2)}) collective-permute-start(bf16[1,256,256]{1,2,0:T(8,128)(2,1)S(1)} %get-tuple-element.188), channel_id=1, source_target_pairs={{0,1},{1,2},{2,3},{3,0},{4,5},{5,6},{6,7},{7,4},{8,9},{9,10},{10,1... | collective-permute-start | bytes 393224 | tf_op jit(solution)/shard_map/ppermute | solution.py:20
  183.1 12.3 %collective-permute-start.4 = (bf16[1,256,256]{1,2,0:T(8,128)(2,1)S(1)}, bf16[1,256,256]{1,2,0:T(8,128)(2,1)S(1)}, u32[]{:S(2)}, u32[]{:S(2)}) collective-permute-start(bf16[1,256,256]{1,2,0:T(8,128)(2,1)S(1)} %get-tuple-element.189), channel_id=1, source_target_pairs={{1,0},{2,1},{3,2},{0,3},{5,4},{6,5},{7,6},{4,7},{9,8},{10,9},{11,1... | collective-permute-start | bytes 393224 | tf_op jit(solution)/shard_map/ppermute | solution.py:21
  195.1 59.6 %reduce-scatter.7.cloned.1.call-start = ((), (), s32[]{:S(2)}) async-start(), calls=%async_computation.6 | async-start | bytes 1474560 | tf_op jit(solution)/shard_map/reduce_scatter | solution.py:133
  203.3 18.4 %copy-start.8 = (bf16[256,1024]{0,1:T(8,128)(2,1)}, bf16[256,1024]{0,1:T(8,128)(2,1)S(1)}, u32[]{:S(2)}) copy-start(bf16[256,1024]{0,1:T(8,128)(2,1)S(1)} %get-tuple-element.118) | copy-start | bytes 1572868
  226.7 88.1 %all-reduce.3.cloned.1.call-start = ((), (), s32[]{:S(2)}) async-start(), calls=%async_computation.9 | async-start | bytes 1769472 | tf_op jit(solution)/shard_map/psum | solution.py:136
  234.2 20.5 %copy-start.9 = (bf16[256,1024]{0,1:T(8,128)(2,1)S(1)}, bf16[256,1024]{0,1:T(8,128)(2,1)}, u32[]{:S(2)}) copy-start(bf16[256,1024]{0,1:T(8,128)(2,1)} %copy-done.8) | copy-start | bytes 1572868
  255.9 61.4 %copy-start.1 = (f32[2,12,64,64]{3,2,1,0:T(8,128)S(1)}, f32[2,12,64,64]{3,2,1,0:T(8,128)}, u32[]{:S(2)}) copy-start(f32[2,12,64,64]{3,2,1,0:T(8,128)} %param.12) | copy-start | bytes 1179652
  (32 other events, 74.1 us)
Sparse Core Ops, SparseCore 0:
  11.3 55.3 reduce-scatter.4
  146.1 27.8 reduce-scatter.10
  195.2 27.7 reduce-scatter.8
  226.9 27.7 reduce-scatter.6
  257.3 57.5 all-reduce.2
